TPU v7x, 256 devices: a whole 4x4x8 slice. The times are simulated.
256 devices in a mesh: rows: 64 (over x, z, core), cols: 4 (over y).
Axes of the slice: x: 4, y: 4, z: 8, core: 2. Of those that a mesh axis runs over, the one named last changes fastest.
Arguments:
- slot_tile: int32 [64, 3], replicated, may hold values from 0 to 128, as said below
- slot_ranks: int32 [64, 3, 4], P('rows', None, 'cols'), may hold values from 0 to 256, as said below
- diag_ranks: int32 [4], P('cols'), may hold values from 32 to 256
- panel_left_factors: bfloat16 [4, 192, 1024, 256], P('cols', 'rows'), may hold values from -12 to 12
- panel_v: bfloat16 [4, 192, 1024, 256], P('cols', 'rows'), may hold values from -0.1875 to 0.1875
- diag_u: bfloat16 [4, 1024, 256], P('cols'), may hold values from -0.38 to 0.38, as said below
- diag_v: bfloat16 [4, 1024, 256], P('cols'), may hold values from -1 to 1
- panel_points: int32 [192, 2, 1024], P('rows', None, 'cols'), may hold values from 0 to 1023, as said below
- diag_points: int32 [2, 1024], replicated, may hold values from 0 to 1023, as said below
- rhs_diag: float32 [1024, 512], P(None, 'cols'), may hold values from -0.3 to 0.3
- rhs_rest: float32 [128, 4, 4, 64, 512], P(None, 'cols', None, 'rows'), may hold values from -6 to 6
Outputs:
- panel_factor: bfloat16 [192, 1024, 1024], P('rows', 'cols')
- diag_solution: float32 [1024, 512], P(None, 'cols')
- rhs_out: float32 [128, 4, 4, 64, 512], P(None, 'cols', None, 'rows')
Inputs may be any that keep to these rules, and one draw needn't show every extreme that they name: `slot_tile`: every tile 0 to 127 stands in exactly one slot; 128 marks an empty slot; the live slots of an owner come first; every owner has 1 to 3 live slots and some owner has 3. Owners are chosen by the tiles' summed ranks. `slot_ranks`: live slots have ranks 32 to 256, empty slots 0; both 32 and 256 occur. The columns of each diag_u[j] are orthogonal, with lengths 0.1 to 0.38. `panel_points`: row 0 holds x, row 1 holds y. A live slot holds the cells of a block of 32 x (32) grid cells in some order; blocks of different tiles and of the diagonal tile are distinct; an empty slot holds the points of some tile. `diag_points`: row 0 holds x, row 1 holds y: the cells of one block of 32 x (32) grid cells in some order.
All inputs are finite; a program needn't handle non-finite values.
Results may differ from a plain program's by a relative error of at most 0.0057.
Values may be sent and summed in bfloat16 or wider, within the bound.
A program may use at most 128 MiB of HBM per device.

v0:
```python
import jax
import jax.numpy as jnp
from jax import lax
from jax.sharding import PartitionSpec as P

GX = 1024
length_scale = 0.3
nugget = 1.0


def matern(first_x, first_y, second_x, second_y):
    spacing = 1.0 / GX
    delta_x = (first_x - second_x) * spacing
    delta_y = (first_y - second_y) * spacing
    scaled = jnp.sqrt(3.0) * jnp.sqrt(delta_x * delta_x + delta_y * delta_y) / length_scale
    return (1.0 + scaled) * jnp.exp(-scaled)


def owner_rows(slot_tile, tile_count, per_peer, row_devices):
    flat_tiles = slot_tile.reshape(-1)
    slot_count = flat_tiles.shape[0]
    tmax_local = slot_tile.shape[1]
    owner_slot = (
        jnp.zeros((tile_count + 1,), jnp.int32)
        .at[flat_tiles]
        .set(jnp.arange(slot_count, dtype=jnp.int32))[:tile_count]
    )
    source_row = owner_slot // tmax_local
    source_place = owner_slot % tmax_local
    step_index = jnp.arange(per_peer, dtype=jnp.int32)
    return (
        (source_place[:, None] * per_peer + step_index[None, :]) * row_devices + source_row[:, None]
    ).reshape(-1)


def times_block(owned_rows, forward):
    return jnp.dot(
        owned_rows,
        lax.all_gather(forward, "cols", axis=1, tiled=True),
        preferred_element_type=jnp.float32,
    )


def per_device(
    slot_tile,
    slot_ranks,
    diag_ranks,
    panel_left_factors,
    panel_v,
    diag_u,
    diag_v,
    panel_points,
    diag_points,
    rhs_diag,
    rhs_rest,
):
    row_devices = lax.axis_size("rows")
    col_devices = lax.axis_size("cols")
    slot_count = panel_left_factors.shape[1]
    tile_order = diag_u.shape[1]
    rank_max = diag_u.shape[2]
    quarter = tile_order // col_devices
    per_peer = quarter // row_devices
    tile_count = rhs_rest.shape[0]
    row_index = lax.axis_index("rows")
    rank_index = jnp.arange(rank_max, dtype=jnp.int32)
    diag_mask = (rank_index < diag_ranks[0]).astype(jnp.bfloat16)
    diagonal_left_factor = diag_u[0] * diag_mask[None, :]
    diagonal_right_factor = diag_v[0] * diag_mask[None, :]
    slot_mask = (rank_index[None, :] < slot_ranks[0, :, 0][:, None]).astype(jnp.bfloat16)
    slot_left_factor = panel_left_factors[0] * slot_mask[:, None, :]
    slot_right_factor = panel_v[0] * slot_mask[:, None, :]
    inner_product_core = jnp.einsum(
        "gok,oe->gke", slot_right_factor, diagonal_right_factor, preferred_element_type=jnp.float32
    ).astype(jnp.bfloat16)
    low_rows = jnp.einsum(
        "lgc,lcz->lgz", slot_left_factor, inner_product_core, preferred_element_type=jnp.float32
    ).astype(jnp.bfloat16)
    diag_core = jnp.einsum(
        "br,bq->rq",
        diagonal_right_factor,
        diagonal_right_factor,
        preferred_element_type=jnp.float32,
    ).astype(jnp.bfloat16)
    diag_low = jnp.dot(diagonal_left_factor, diag_core, preferred_element_type=jnp.float32).astype(
        jnp.bfloat16
    )
    gathered_low, gathered_left = (
        lax.all_gather(diag_low[None], "cols", axis=0, tiled=True),
        lax.all_gather(diagonal_left_factor[None], "cols", axis=0, tiled=True),
    )
    outgoing_low = low_rows.reshape(slot_count, col_devices, quarter, rank_max)
    update_term = jnp.einsum(
        "sjnr,jbr->snb",
        lax.all_to_all(outgoing_low, "cols", split_axis=1, concat_axis=1, tiled=True),
        gathered_left,
        preferred_element_type=jnp.float32,
    )
    centre = diag_points.astype(jnp.float32)
    identity = jnp.eye(tile_order, dtype=jnp.float32)
    diag_term = jnp.einsum(
        "jbr,jcr->bc", gathered_low, gathered_left, preferred_element_type=jnp.float32
    )
    own_block = matern(centre[0][:, None], centre[1][:, None], centre[0], centre[1])
    diag_system = own_block + nugget * identity - diag_term
    factor = jnp.linalg.cholesky(diag_system)
    inverse = jax.scipy.linalg.solve_triangular(factor, identity, lower=True)
    my_tiles = lax.dynamic_slice_in_dim(slot_tile, row_index, 1, 0)[0]
    live_mask = (my_tiles < tile_count).astype(jnp.float32)
    coords = panel_points.astype(jnp.float32)
    generated = matern(coords[:, 0, :, None], coords[:, 1, :, None], centre[0], centre[1])
    system_rows = live_mask[:, None, None] * (generated - update_term)
    panel_factor = jnp.einsum(
        "snb,cb->snc", system_rows, inverse, precision=lax.Precision.HIGHEST
    ).astype(jnp.bfloat16)
    diag_solution = jnp.dot(inverse, rhs_diag, precision=lax.Precision.HIGHEST)
    forward = diag_solution.astype(jnp.bfloat16)
    pick_rows = owner_rows(slot_tile, tile_count, per_peer, row_devices)
    outgoing_rows = panel_factor.reshape(slot_count, per_peer, row_devices, tile_order)
    incoming = lax.all_to_all(outgoing_rows, "rows", split_axis=2, concat_axis=2, tiled=True)
    owned_rows = jnp.take(incoming.reshape(-1, tile_order), pick_rows, axis=0)
    product = times_block(owned_rows, forward).astype(jnp.bfloat16)
    rhs_out = rhs_rest - product.reshape(rhs_rest.shape).astype(jnp.float32)
    return (panel_factor, diag_solution, rhs_out)


def solution(mesh):
    return jax.shard_map(
        per_device,
        mesh=mesh,
        in_specs=(
            P(),
            P("rows", None, "cols"),
            P("cols"),
            P("cols", "rows", None, None),
            P("cols", "rows", None, None),
            P("cols", None, None),
            P("cols", None, None),
            P("rows", None, "cols"),
            P(),
            P(None, "cols"),
            P(None, "cols", None, "rows", None),
        ),
        out_specs=(P("rows", "cols", None), P(None, "cols"), P(None, "cols", None, "rows", None)),
        check_vma=False,
    )
```

profile of v0, /device:TPU:1, one launch (start us, length us, event | category | flops | bytes accessed | tf_op | source)
XLA Modules:
  0.0 559.6 jit_solution(14840995524542032224)
XLA Ops:
  10.0 3.0 convolution_convert_fusion.1
  13.1 3.7 convolution_convert_fusion
  18.1 5.0 all-to-all-start
  24.6 2.4 fusion.42
  27.1 34.0 %all-gather.5.cloned.1.call-done = bf16[4,1024,256]{2,1,0:T(8,128)(2,1)} async-done(((bf16[1,1024,256]{2,1,0:T(8,128)(2,1)}), bf16[4,1024,256]{2,1,0:T(8,128)(2,1)}) %all-gather.5.cloned.1.call-update) | async-done | bytes 2097168 | tf_op jit(solution)/shard_map/all_gather | solution.py:90
  61.1 36.7 %all-gather.9.cloned.1.call-done = bf16[4096,256]{1,0:T(8,128)(2,1)} async-done(((bf16[1024,256]{1,0:T(8,128)(2,1)}), bf16[4096,256]{1,0:T(8,128)(2,1)}) %all-gather.9.cloned.1.call-update) | async-done | bytes 2097168 | tf_op jit(solution)/shard_map/all_gather | solution.py:89
  97.8 6.6 %convolution_bitcast_fusion = f32[1024,1024]{1,0:T(8,128)} fusion(bf16[4,1024,256]{2,1,0:T(8,128)(2,1)} %bitcast.174, bf16[4,1024,256]{2,1,0:T(8,128)(2,1)} %all-gather.5.cloned.1.call-done), kind=kOutput, calls=%fused_computation.28 | convolution fusion | flops 2147483648 | bytes 8388608 | tf_op jit(solution)/shard_map/jbr,jcr->bc/dot_general | solution.py:101
  104.4 5.3 copy.22
  109.7 9.6 %fusion.3 = f32[1024,1024]{1,0:T(8,128)S(1)} fusion(f32[1024,1024]{0,1:T(8,128)} %copy.22, f32[1024,1024]{1,0:T(8,128)} %convolution_bitcast_fusion, f32[1024]{0:T(1024)S(1)} %bitcast.169, f32[1024]{0:T(1024)S(1)} %bitcast.167), kind=kLoop, calls=%fused_computation.9 | loop fusion | flops 33554432 | bytes 12591104 | tf_op jit(solution)/shard_map/jit(cholesky)/div | solution.py:106
  121.3 11.7 %cholesky.224 = f32[128,128]{1,0:T(8,128)S(1)} custom-call(f32[128,128]{1,0:T(8,128)S(1)} %cholesky.583), custom_call_target="Cholesky" | custom-call | tf_op jit(solution)/shard_map/jit(cholesky)/cholesky | solution.py:106
  133.0 9.8 %custom-call.63 = f32[1,128,128]{1,2,0:T(8,128)S(1)} custom-call(f32[1,128,128]{2,1,0:T(8,128)S(1)} %get-tuple-element.67), custom_call_target="InvertDiagBlocksLowerTriangular" | custom-call | tf_op jit(solution)/shard_map/jit(cholesky)/cholesky | solution.py:106
  142.9 2.5 cholesky.256
  149.3 11.7 %cholesky.245 = f32[128,128]{1,0:T(8,128)S(1)} custom-call(f32[128,128]{1,0:T(8,128)S(1)} %cholesky.587), custom_call_target="Cholesky" | custom-call | tf_op jit(solution)/shard_map/jit(cholesky)/cholesky | solution.py:106
  161.6 10.2 %custom-call.64 = f32[1,128,128]{1,2,0:T(8,128)S(1)} custom-call(f32[1,128,128]{2,1,0:T(8,128)S(1)} %get-tuple-element.64), custom_call_target="InvertDiagBlocksLowerTriangular" | custom-call | tf_op jit(solution)/shard_map/jit(cholesky)/cholesky | solution.py:106
  175.2 11.7 %cholesky.470 = f32[128,128]{1,0:T(8,128)S(1)} custom-call(f32[128,128]{1,0:T(8,128)S(1)} %cholesky.592), custom_call_target="Cholesky" | custom-call | tf_op jit(solution)/shard_map/jit(cholesky)/cholesky | solution.py:106
  188.3 9.8 %custom-call.65 = f32[1,128,128]{1,2,0:T(8,128)S(1)} custom-call(f32[1,128,128]{2,1,0:T(8,128)S(1)} %get-tuple-element.61), custom_call_target="InvertDiagBlocksLowerTriangular" | custom-call | tf_op jit(solution)/shard_map/jit(cholesky)/cholesky | solution.py:106
  201.6 11.9 %cholesky.489 = f32[128,128]{1,0:T(8,128)S(1)} custom-call(f32[128,128]{1,0:T(8,128)S(1)} %cholesky.597), custom_call_target="Cholesky" | custom-call | tf_op jit(solution)/shard_map/jit(cholesky)/cholesky | solution.py:106
  214.8 9.8 %custom-call.66 = f32[1,128,128]{1,2,0:T(8,128)S(1)} custom-call(f32[1,128,128]{2,1,0:T(8,128)S(1)} %get-tuple-element.58), custom_call_target="InvertDiagBlocksLowerTriangular" | custom-call | tf_op jit(solution)/shard_map/jit(cholesky)/cholesky | solution.py:106
  228.1 11.7 %cholesky.508 = f32[128,128]{1,0:T(8,128)S(1)} custom-call(f32[128,128]{1,0:T(8,128)S(1)} %cholesky.602), custom_call_target="Cholesky" | custom-call | tf_op jit(solution)/shard_map/jit(cholesky)/cholesky | solution.py:106
  241.1 9.8 %custom-call.67 = f32[1,128,128]{1,2,0:T(8,128)S(1)} custom-call(f32[1,128,128]{2,1,0:T(8,128)S(1)} %get-tuple-element.55), custom_call_target="InvertDiagBlocksLowerTriangular" | custom-call | tf_op jit(solution)/shard_map/jit(cholesky)/cholesky | solution.py:106
  251.9 2.5 convolution_subtract_fusion.9
  254.4 11.7 %cholesky.528 = f32[128,128]{1,0:T(8,128)S(1)} custom-call(f32[128,128]{1,0:T(8,128)S(1)} %cholesky.607), custom_call_target="Cholesky" | custom-call | tf_op jit(solution)/shard_map/jit(cholesky)/cholesky | solution.py:106
  267.5 9.8 %custom-call.68 = f32[1,128,128]{1,2,0:T(8,128)S(1)} custom-call(f32[1,128,128]{2,1,0:T(8,128)S(1)} %get-tuple-element.52), custom_call_target="InvertDiagBlocksLowerTriangular" | custom-call | tf_op jit(solution)/shard_map/jit(cholesky)/cholesky | solution.py:106
  280.3 11.7 %cholesky.548 = f32[128,128]{1,0:T(8,128)S(1)} custom-call(f32[128,128]{1,0:T(8,128)S(1)} %cholesky.612), custom_call_target="Cholesky" | custom-call | tf_op jit(solution)/shard_map/jit(cholesky)/cholesky | solution.py:106
  293.3 10.2 %custom-call.69 = f32[1,128,128]{1,2,0:T(8,128)S(1)} custom-call(f32[1,128,128]{2,1,0:T(8,128)S(1)} %get-tuple-element.49), custom_call_target="InvertDiagBlocksLowerTriangular" | custom-call | tf_op jit(solution)/shard_map/jit(cholesky)/cholesky | solution.py:106
  306.2 11.7 %cholesky.566 = f32[128,128]{1,0:T(8,128)S(1)} custom-call(f32[128,128]{1,0:T(8,128)S(1)} %convolution_subtract_fusion.11), custom_call_target="Cholesky" | custom-call | tf_op jit(solution)/shard_map/jit(cholesky)/cholesky | solution.py:106
  324.9 4.8 select_select_fusion
  329.7 27.4 %while.1 = (s32[]{:T(128)}, f32[1024,1024]{1,0:T(8,128)}, s32[8,2]{0,1:T(2,128)S(1)}, f32[8,128,128]{2,1,0:T(8,128)}, s32[]{:T(128)}) while((s32[]{:T(128)}, f32[1024,1024]{1,0:T(8,128)}, s32[8,2]{0,1:T(2,128)S(1)}, f32[8,128,128]{2,1,0:T(8,128)}, s32[]{:T(128)}) %tuple.66), condition=%wide.while_cond, body=%wide.while_body.sunk | while | flops 2 | bytes 132705 | solution.py:107
  330.3 2.8 bitcast_dynamic-update-slice_fusion.2
  333.8 2.8 bitcast_dynamic-update-slice_fusion.2
  337.2 2.9 bitcast_dynamic-update-slice_fusion.2
  340.6 2.8 bitcast_dynamic-update-slice_fusion.2
  344.1 2.8 bitcast_dynamic-update-slice_fusion.2
  347.5 2.8 bitcast_dynamic-update-slice_fusion.2
  350.9 2.8 bitcast_dynamic-update-slice_fusion.2
  354.4 2.8 bitcast_dynamic-update-slice_fusion.2
  357.1 79.6 %custom-call.70 = f32[8,128,128]{1,2,0:T(8,128)S(1)} custom-call(f32[8,128,128]{2,1,0:T(8,128)} %get-tuple-element.10), custom_call_target="InvertDiagBlocksLowerTriangular" | custom-call | tf_op jit(solution)/shard_map/jit(_solve_triangular)/triangular_solve | solution.py:107
  452.8 2.6 convolution_subtract_fusion.2
  457.0 2.8 convolution_subtract_fusion.1
  461.2 3.5 convolution_subtract_fusion.3
  466.2 3.4 fusion.27
  469.6 16.3 %fusion.29 = bf16[3,256,1024]{2,1,0:T(8,128)(2,1)S(1)} fusion(f32[1024,1024]{1,0:T(8,128)} %convolution_dynamic-update-slice_fusion, f32[3,256,1024,1]{2,1,0,3:T(8,128)S(1)} %fusion.27, f32[1024]{0:T(1024)S(1)} %bitcast.170, f32[3,256]{1,0:T(4,128)S(1)} %get-tuple-element.84, f32[1024]{0:T(1024)S(1)} %bitcast.168, f32[3,256]{1,0:T(4,128)S(1)} %get-tuple-element.85, ...), kind=kOutput, calls=%fused_computation.40 | convolution fusion | flops 9674686464 | bytes 8927244 | tf_op jit(solution)/shard_map/snb,cb->snc/dot_general | solution.py:113
  489.4 11.0 %all-to-all-start.1 = ((bf16[3,4,64,1024]{3,1,0,2:T(4,128)(2,1)}), bf16[3,4,64,1024]{3,1,0,2:T(4,128)(2,1)}, u32[]{:S(2)}, u32[]{:S(2)}) async-start(bf16[3,4,64,1024]{3,1,0,2:T(4,128)(2,1)} %copy.24), calls=%async_computation.1 | async-start | bytes 3145728 | tf_op jit(solution)/shard_map/all_to_all | solution.py:120
  500.7 6.5 %fusion.142 = (bf16[1024,128]{1,0:T(8,128)(2,1)}, f32[1024,128]{1,0:T(8,128)}) fusion(f32[1024,1024]{1,0:T(8,128)} %convolution_dynamic-update-slice_fusion, f32[1024,128]{1,0:T(8,128)S(1)} %copy-done), kind=kOutput, calls=%fused_computation.240 | convolution fusion | flops 1610743808 | bytes 5505024 | tf_op jit(solution)/shard_map/dot_general | solution.py:116
  509.0 31.1 %all-to-all-done.1 = bf16[3,4,64,1024]{3,1,0,2:T(4,128)(2,1)} async-done(((bf16[3,4,64,1024]{3,1,0,2:T(4,128)(2,1)}), bf16[3,4,64,1024]{3,1,0,2:T(4,128)(2,1)}, u32[]{:S(2)}, u32[]{:S(2)}) %all-to-all-start.1) | async-done | bytes 1572896 | tf_op jit(solution)/shard_map/all_to_all | solution.py:120
  541.9 2.8 gather_fusion
  544.7 3.4 fusion.52
  548.1 2.5 reshape.321
  (120 shorter events, 71.7 us)
Async XLA Ops:
  7.2 493.5 %copy-start = (f32[1024,128]{1,0:T(8,128)S(1)}, f32[1024,128]{1,0:T(8,128)}, u32[]{:S(2)}) copy-start(f32[1024,128]{1,0:T(8,128)} %param.20) | copy-start | bytes 1572868
  7.2 5.9 %copy-start.9 = (bf16[1,1024,256]{2,1,0:T(8,128)(2,1)S(1)}, bf16[1,1024,256]{2,1,0:T(8,128)(2,1)}, u32[]{:S(2)}) copy-start(bf16[1,1024,256]{2,1,0:T(8,128)(2,1)} %param.17) | copy-start | bytes 1572868
  7.2 5.8 %copy-start.8 = (s32[1,3,1]{1,2,0:T(1,128)S(1)}, s32[1,3,1]{1,2,0:T(1,128)}, u32[]{:S(2)}) copy-start(s32[1,3,1]{1,2,0:T(1,128)} %param.12) | copy-start | bytes 40
  7.2 53.9 %all-gather.5.cloned.1.call-start = ((), (), s32[]{:S(2)}) async-start(), calls=%async_computation.2 | async-start | bytes 2621440 | tf_op jit(solution)/shard_map/all_gather | solution.py:90
  9.9 87.9 %all-gather.9.cloned.1.call-start = ((), (), s32[]{:S(2)}) async-start(), calls=%async_computation.4 | async-start | bytes 2621440 | tf_op jit(solution)/shard_map/all_gather | solution.py:89
  16.8 6.3 %copy-start.6 = (s32[2,1024]{1,0:T(2,128)S(1)}, s32[2,1024]{1,0:T(2,128)}, u32[]{:S(2)}) copy-start(s32[2,1024]{1,0:T(2,128)} %param.19) | copy-start | bytes 24580
  16.8 6.3 %copy-start.7 = (s32[3,2,256]{2,1,0:T(2,128)S(1)}, s32[3,2,256]{2,1,0:T(2,128)}, u32[]{:S(2)}) copy-start(s32[3,2,256]{2,1,0:T(2,128)} %param.18) | copy-start | bytes 18436
  16.8 6.3 %copy-start.5 = (s32[64,3]{0,1:T(4,128)S(1)}, s32[64,3]{0,1:T(4,128)}, u32[]{:S(2)}) copy-start(s32[64,3]{0,1:T(4,128)} %param.11) | copy-start | bytes 2308
  18.1 448.1 %all-to-all-start = ((bf16[3,4,256,256]{3,2,0,1:T(8,128)(2,1)}), bf16[3,4,256,256]{3,2,0,1:T(8,128)(2,1)S(1)}, u32[]{:S(2)}, u32[]{:S(2)}) async-start(bf16[3,4,256,256]{3,2,0,1:T(8,128)(2,1)} %copy.20), calls=%async_computation | async-start | bytes 3145728 | tf_op jit(solution)/shard_map/all_to_all | solution.py:95
  119.3 2.0 copy-start.2
  436.7 5.6 %copy-start.1 = (f32[1024,1024]{1,0:T(8,128)S(1)}, f32[1024,1024]{1,0:T(8,128)}, u32[]{:S(2)}) copy-start(f32[1024,1024]{1,0:T(8,128)} %fusion.42) | copy-start | bytes 12582916
  485.9 1.1 copy-start.3
  489.4 50.7 %all-to-all-start.1 = ((bf16[3,4,64,1024]{3,1,0,2:T(4,128)(2,1)}), bf16[3,4,64,1024]{3,1,0,2:T(4,128)(2,1)}, u32[]{:S(2)}, u32[]{:S(2)}) async-start(bf16[3,4,64,1024]{3,1,0,2:T(4,128)(2,1)} %copy.24), calls=%async_computation.1 | async-start | bytes 3145728 | tf_op jit(solution)/shard_map/all_to_all | solution.py:120
  500.4 44.4 %all-gather.7.cloned.1.call-start = ((), (), s32[]{:S(2)}) async-start(), calls=%async_computation.3 | async-start | bytes 1310720 | tf_op jit(solution)/shard_map/all_gather | solution.py:39
  544.7 5.9 %copy-start.4 = (f32[128,1,4,1,512]{4,3,2,1,0:T(1,128)S(1)}, f32[128,1,4,1,512]{4,3,2,1,0:T(1,128)}, u32[]{:S(2)}) copy-start(f32[128,1,4,1,512]{4,3,2,1,0:T(1,128)} %param.21) | copy-start | bytes 3145732
Sparse Core Ops, SparseCore 0:
  10.0 51.0 all-gather.4
  63.5 34.2 all-gather.8
  507.3 26.3 all-gather.6
where the time goes:
time: 567 us; the launch traced here: 560 us
  other arithmetic  275 us (49%)
  waiting for transfers between devices  102 us (18%)
  matrix products  95.5 us (17%)
  local copies, waits for them, and re-layouts  50.8 us (9%)
  between operations  20.4 us (4%)
  starting transfers between devices  16.4 us (3%)
    another operation x30, other arithmetic, per_device(): factor = jnp.linalg.cholesky(diag_system)  172 us
    another operation x3, other arithmetic, per_device(): inverse = jax.scipy.linalg.solve_triangular(factor, identity, lower=True)  84.4 us
    all_gather x1, waiting for transfers between devices, per_device(): lax.all_gather(diag_low[None], 'cols', axis=0, tiled=True)  36.7 us
    all_gather x1, waiting for transfers between devices, per_device(): lax.all_gather(diagonal_left_factor[None], 'cols', axis=0, tiled=True)  34 us
    all_to_all x1, waiting for transfers between devices, per_device(): lax.all_to_all(outgoing_rows, 'rows', split_axis=2, concat_axis=2, tiled=...  31.1 us
    another operation x15, matrix products, per_device(): inverse = jax.scipy.linalg.solve_triangular(factor, identity, lower=True)  29.4 us
    another operation x24, local copies, waits for them, and re-layouts  27.4 us
    another operation x14, matrix products, per_device(): factor = jnp.linalg.cholesky(diag_system)  23.3 us
  transfers between devices with their start and end apart: 5, of which 3 were waited for; matrix products, arithmetic and copies ran while one was open for 69% of the time, Pallas kernels for 0%

commit v1 on v0

--- a/solution.py
+++ b/solution.py
@@ -86,7 +86,10 @@
         jnp.bfloat16
     )
     gathered_low, gathered_left = (
-        lax.all_gather(diag_low[None], "cols", axis=0, tiled=True),
+        jnp.concatenate(
+            lax.all_to_all(jnp.stack([diag_low[None]] * lax.axis_size("cols")), "cols", 0, 0),
+            axis=0,
+        ),
         lax.all_gather(diagonal_left_factor[None], "cols", axis=0, tiled=True),
     )
     outgoing_low = low_rows.reshape(slot_count, col_devices, quarter, rank_max)

time: 567 us -> 538 us (0.949)
  waiting for transfers between devices: 102 us -> 58.6 us
  starting transfers between devices: 16.4 us -> 26.3 us
    all_gather x1 -> x0, waiting for transfers between devices: 36.7 us -> none  [per_device(): lax.all_gather(diag_low[None], 'cols', axis=0, tiled=True)]
    all_gather x1, waiting for transfers between devices: 34 us -> 2.16 us  [per_device(): lax.all_gather(diagonal_left_factor[None], 'cols', axis=0, tiled=True)]
    all_to_all x0 -> x1, waiting for transfers between devices: none -> 25.3 us  [per_device(): lax.all_to_all(jnp.stack([diag_low[None]] * lax.axis_size('cols')), 'cols...]
    all_to_all x1, starting transfers between devices: 11 us -> 16.7 us  [per_device(): lax.all_to_all(outgoing_rows, 'rows', split_axis=2, concat_axis=2, tiled=...]
    another operation x24 -> x25, local copies, waits for them, and re-layouts: 27.4 us -> 29.4 us
  transfers between devices with their start and end apart: 5 -> 5, of which waited for: 3 -> 3; matrix products, arithmetic and copies ran while one was open for 69% -> 73% of each run, Pallas kernels for 0% -> 0%
where the time goes in v1:
time: 538 us; the launch traced here: 530 us
  other arithmetic  274 us (51%)
  matrix products  95.8 us (18%)
  waiting for transfers between devices  58.6 us (11%)
  local copies, waits for them, and re-layouts  54.3 us (10%)
  starting transfers between devices  26.3 us (5%)
  between operations  20.7 us (4%)
    another operation x30, other arithmetic, per_device(): factor = jnp.linalg.cholesky(diag_system)  172 us
    another operation x3, other arithmetic, per_device(): inverse = jax.scipy.linalg.solve_triangular(factor, identity, lower=True)  84.4 us
    all_to_all x1, waiting for transfers between devices, per_device(): lax.all_to_all(outgoing_rows, 'rows', split_axis=2, concat_axis=2, tiled=...  31.1 us
    another operation x15, matrix products, per_device(): inverse = jax.scipy.linalg.solve_triangular(factor, identity, lower=True)  29.4 us
    another operation x24, local copies, waits for them, and re-layouts  28 us
    all_to_all x1, waiting for transfers between devices, per_device(): lax.all_to_all(jnp.stack([diag_low[None]] * lax.axis_size('cols')), 'cols...  25.3 us
    another operation x14, matrix products, per_device(): factor = jnp.linalg.cholesky(diag_system)  23.3 us
    all_to_all x1, starting transfers between devices, per_device(): lax.all_to_all(outgoing_rows, 'rows', split_axis=2, concat_axis=2, tiled=...  16.7 us
  transfers between devices with their start and end apart: 5, of which 3 were waited for; matrix products, arithmetic and copies ran while one was open for 73% of the time, Pallas kernels for 0%

profile of v1, /device:TPU:1, one launch (start us, length us, event | category | flops | bytes accessed | tf_op | source)
XLA Modules:
  0.0 530.2 jit_solution(14962753936765922332)
XLA Ops:
  13.6 5.0 all-to-all-start.1
  18.7 4.9 convolution_convert_fusion
  23.6 2.7 copy.20
  27.8 2.4 fusion.43
  30.3 25.3 %all-to-all-done.1 = bf16[4,1,1024,256]{3,2,1,0:T(8,128)(2,1)S(1)} async-done(((bf16[4,1,1024,256]{3,2,1,0:T(8,128)(2,1)}), bf16[4,1,1024,256]{3,2,1,0:T(8,128)(2,1)S(1)}, u32[]{:S(2)}, u32[]{:S(2)}) %all-to-all-start.1) | async-done | bytes 2097184 | tf_op jit(solution)/shard_map/all_to_all | solution.py:90
  55.6 4.3 all-to-all-start
  62.1 5.9 %convolution_bitcast_fusion = f32[1024,1024]{1,0:T(8,128)} fusion(bf16[4,1024,256]{2,1,0:T(8,128)(2,1)} %all-gather.3.cloned.1.call-done, bf16[4,1,1024,256]{3,2,1,0:T(8,128)(2,1)S(1)} %all-to-all-done.1), kind=kOutput, calls=%fused_computation.28 | convolution fusion | flops 2147483648 | bytes 8388608 | tf_op jit(solution)/shard_map/jbr,jcr->bc/dot_general | solution.py:104
  68.0 5.3 %copy.22 = f32[1024,1024]{0,1:T(8,128)} copy(f32[1024,1024]{1,0:T(8,128)} %convolution_bitcast_fusion) | data formatting | bytes 8388608 | tf_op jit(solution)/shard_map/jbr,jcr->bc/dot_general | solution.py:104
  73.4 9.6 %fusion.3 = f32[1024,1024]{1,0:T(8,128)S(1)} fusion(f32[1024,1024]{0,1:T(8,128)} %copy.22, f32[1024,1024]{1,0:T(8,128)} %convolution_bitcast_fusion, f32[1024]{0:T(1024)S(1)} %bitcast.170, f32[1024]{0:T(1024)S(1)} %bitcast.168), kind=kLoop, calls=%fused_computation.9 | loop fusion | flops 33554432 | bytes 12591104 | tf_op jit(solution)/shard_map/jit(cholesky)/div | solution.py:109
  84.9 11.7 %cholesky.224 = f32[128,128]{1,0:T(8,128)S(1)} custom-call(f32[128,128]{1,0:T(8,128)S(1)} %cholesky.583), custom_call_target="Cholesky" | custom-call | tf_op jit(solution)/shard_map/jit(cholesky)/cholesky | solution.py:109
  96.7 9.8 %custom-call.63 = f32[1,128,128]{1,2,0:T(8,128)S(1)} custom-call(f32[1,128,128]{2,1,0:T(8,128)S(1)} %get-tuple-element.67), custom_call_target="InvertDiagBlocksLowerTriangular" | custom-call | tf_op jit(solution)/shard_map/jit(cholesky)/cholesky | solution.py:109
  106.5 2.5 cholesky.256
  112.9 11.7 %cholesky.245 = f32[128,128]{1,0:T(8,128)S(1)} custom-call(f32[128,128]{1,0:T(8,128)S(1)} %cholesky.587), custom_call_target="Cholesky" | custom-call | tf_op jit(solution)/shard_map/jit(cholesky)/cholesky | solution.py:109
  125.3 10.2 %custom-call.64 = f32[1,128,128]{1,2,0:T(8,128)S(1)} custom-call(f32[1,128,128]{2,1,0:T(8,128)S(1)} %get-tuple-element.64), custom_call_target="InvertDiagBlocksLowerTriangular" | custom-call | tf_op jit(solution)/shard_map/jit(cholesky)/cholesky | solution.py:109
  138.8 11.7 %cholesky.470 = f32[128,128]{1,0:T(8,128)S(1)} custom-call(f32[128,128]{1,0:T(8,128)S(1)} %cholesky.592), custom_call_target="Cholesky" | custom-call | tf_op jit(solution)/shard_map/jit(cholesky)/cholesky | solution.py:109
  151.8 9.8 %custom-call.65 = f32[1,128,128]{1,2,0:T(8,128)S(1)} custom-call(f32[1,128,128]{2,1,0:T(8,128)S(1)} %get-tuple-element.61), custom_call_target="InvertDiagBlocksLowerTriangular" | custom-call | tf_op jit(solution)/shard_map/jit(cholesky)/cholesky | solution.py:109
  165.2 11.9 %cholesky.489 = f32[128,128]{1,0:T(8,128)S(1)} custom-call(f32[128,128]{1,0:T(8,128)S(1)} %cholesky.597), custom_call_target="Cholesky" | custom-call | tf_op jit(solution)/shard_map/jit(cholesky)/cholesky | solution.py:109
  178.4 9.8 %custom-call.66 = f32[1,128,128]{1,2,0:T(8,128)S(1)} custom-call(f32[1,128,128]{2,1,0:T(8,128)S(1)} %get-tuple-element.58), custom_call_target="InvertDiagBlocksLowerTriangular" | custom-call | tf_op jit(solution)/shard_map/jit(cholesky)/cholesky | solution.py:109
  191.7 11.7 %cholesky.508 = f32[128,128]{1,0:T(8,128)S(1)} custom-call(f32[128,128]{1,0:T(8,128)S(1)} %cholesky.602), custom_call_target="Cholesky" | custom-call | tf_op jit(solution)/shard_map/jit(cholesky)/cholesky | solution.py:109
  204.7 9.8 %custom-call.67 = f32[1,128,128]{1,2,0:T(8,128)S(1)} custom-call(f32[1,128,128]{2,1,0:T(8,128)S(1)} %get-tuple-element.55), custom_call_target="InvertDiagBlocksLowerTriangular" | custom-call | tf_op jit(solution)/shard_map/jit(cholesky)/cholesky | solution.py:109
  215.6 2.5 convolution_subtract_fusion.9
  218.1 11.7 %cholesky.528 = f32[128,128]{1,0:T(8,128)S(1)} custom-call(f32[128,128]{1,0:T(8,128)S(1)} %cholesky.607), custom_call_target="Cholesky" | custom-call | tf_op jit(solution)/shard_map/jit(cholesky)/cholesky | solution.py:109
  231.2 9.8 %custom-call.68 = f32[1,128,128]{1,2,0:T(8,128)S(1)} custom-call(f32[1,128,128]{2,1,0:T(8,128)S(1)} %get-tuple-element.52), custom_call_target="InvertDiagBlocksLowerTriangular" | custom-call | tf_op jit(solution)/shard_map/jit(cholesky)/cholesky | solution.py:109
  244.0 11.7 %cholesky.548 = f32[128,128]{1,0:T(8,128)S(1)} custom-call(f32[128,128]{1,0:T(8,128)S(1)} %cholesky.612), custom_call_target="Cholesky" | custom-call | tf_op jit(solution)/shard_map/jit(cholesky)/cholesky | solution.py:109
  256.9 10.2 %custom-call.69 = f32[1,128,128]{1,2,0:T(8,128)S(1)} custom-call(f32[1,128,128]{2,1,0:T(8,128)S(1)} %get-tuple-element.49), custom_call_target="InvertDiagBlocksLowerTriangular" | custom-call | tf_op jit(solution)/shard_map/jit(cholesky)/cholesky | solution.py:109
  269.8 11.7 %cholesky.566 = f32[128,128]{1,0:T(8,128)S(1)} custom-call(f32[128,128]{1,0:T(8,128)S(1)} %convolution_subtract_fusion.11), custom_call_target="Cholesky" | custom-call | tf_op jit(solution)/shard_map/jit(cholesky)/cholesky | solution.py:109
  288.4 4.8 select_select_fusion
  293.3 28.0 %while.1 = (s32[]{:T(128)}, f32[1024,1024]{1,0:T(8,128)}, s32[8,2]{0,1:T(2,128)S(1)}, f32[8,128,128]{2,1,0:T(8,128)}, s32[]{:T(128)}) while((s32[]{:T(128)}, f32[1024,1024]{1,0:T(8,128)}, s32[8,2]{0,1:T(2,128)S(1)}, f32[8,128,128]{2,1,0:T(8,128)}, s32[]{:T(128)}) %tuple.66), condition=%wide.while_cond, body=%wide.while_body.sunk | while | flops 2 | bytes 132705 | solution.py:110
  293.9 2.9 bitcast_dynamic-update-slice_fusion.2
  297.4 2.9 bitcast_dynamic-update-slice_fusion.2
  300.9 2.9 bitcast_dynamic-update-slice_fusion.2
  304.4 2.9 bitcast_dynamic-update-slice_fusion.2
  307.9 2.9 bitcast_dynamic-update-slice_fusion.2
  311.4 2.9 bitcast_dynamic-update-slice_fusion.2
  314.9 2.9 bitcast_dynamic-update-slice_fusion.2
  318.4 2.8 bitcast_dynamic-update-slice_fusion.2
  321.3 79.6 %custom-call.70 = f32[8,128,128]{1,2,0:T(8,128)S(1)} custom-call(f32[8,128,128]{2,1,0:T(8,128)} %get-tuple-element.10), custom_call_target="InvertDiagBlocksLowerTriangular" | custom-call | tf_op jit(solution)/shard_map/jit(_solve_triangular)/triangular_solve | solution.py:110
  417.0 2.6 convolution_subtract_fusion.2
  421.1 2.8 convolution_subtract_fusion.1
  425.4 3.5 convolution_subtract_fusion.3
  430.3 3.9 fusion.27
  434.2 16.3 %fusion.30 = bf16[3,256,1024]{2,1,0:T(8,128)(2,1)S(1)} fusion(f32[1024,1024]{1,0:T(8,128)} %convolution_dynamic-update-slice_fusion, f32[3,256,1024,1]{2,1,0,3:T(8,128)S(1)} %fusion.27, f32[1024]{0:T(1024)S(1)} %bitcast.171, f32[3,256]{1,0:T(4,128)S(1)} %get-tuple-element.84, f32[1024]{0:T(1024)S(1)} %bitcast.169, f32[3,256]{1,0:T(4,128)S(1)} %get-tuple-element.85, ...), kind=kOutput, calls=%fused_computation.41 | convolution fusion | flops 9674686464 | bytes 8927244 | tf_op jit(solution)/shard_map/snb,cb->snc/dot_general | solution.py:116
  454.0 16.7 %all-to-all-start.2 = ((bf16[3,4,64,1024]{3,1,0,2:T(4,128)(2,1)}), bf16[3,4,64,1024]{3,1,0,2:T(4,128)(2,1)}, u32[]{:S(2)}, u32[]{:S(2)}) async-start(bf16[3,4,64,1024]{3,1,0,2:T(4,128)(2,1)} %copy.24), calls=%async_computation.2 | async-start | bytes 3145728 | tf_op jit(solution)/shard_map/all_to_all | solution.py:123
  471.0 6.5 %fusion.143 = (bf16[1024,128]{1,0:T(8,128)(2,1)}, f32[1024,128]{1,0:T(8,128)}) fusion(f32[1024,1024]{1,0:T(8,128)} %convolution_dynamic-update-slice_fusion, f32[1024,128]{1,0:T(8,128)S(1)} %copy-done), kind=kOutput, calls=%fused_computation.241 | convolution fusion | flops 1610743808 | bytes 5505024 | tf_op jit(solution)/shard_map/dot_general | solution.py:119
  479.3 31.1 %all-to-all-done.2 = bf16[3,4,64,1024]{3,1,0,2:T(4,128)(2,1)} async-done(((bf16[3,4,64,1024]{3,1,0,2:T(4,128)(2,1)}), bf16[3,4,64,1024]{3,1,0,2:T(4,128)(2,1)}, u32[]{:S(2)}, u32[]{:S(2)}) %all-to-all-start.2) | async-done | bytes 1572896 | tf_op jit(solution)/shard_map/all_to_all | solution.py:123
  512.2 2.8 gather_fusion
  515.0 3.4 fusion.53
  518.4 2.5 reshape.326
  (120 shorter events, 76.2 us)
Async XLA Ops:
  7.2 463.8 %copy-start = (f32[1024,128]{1,0:T(8,128)S(1)}, f32[1024,128]{1,0:T(8,128)}, u32[]{:S(2)}) copy-start(f32[1024,128]{1,0:T(8,128)} %param.20) | copy-start | bytes 1572868
  7.2 54.9 %all-gather.3.cloned.1.call-start = ((), (), s32[]{:S(2)}) async-start(), calls=%async_computation.3 | async-start | bytes 2621440 | tf_op jit(solution)/shard_map/all_gather | solution.py:93
  9.8 8.8 %copy-start.6 = (s32[2,1024]{1,0:T(2,128)S(1)}, s32[2,1024]{1,0:T(2,128)}, u32[]{:S(2)}) copy-start(s32[2,1024]{1,0:T(2,128)} %param.19) | copy-start | bytes 24580
  9.8 8.8 %copy-start.8 = (s32[1,3,1]{1,2,0:T(1,128)S(1)}, s32[1,3,1]{1,2,0:T(1,128)}, u32[]{:S(2)}) copy-start(s32[1,3,1]{1,2,0:T(1,128)} %param.12) | copy-start | bytes 40
  9.9 8.9 %copy-start.9 = (bf16[1,1024,256]{2,1,0:T(8,128)(2,1)S(1)}, bf16[1,1024,256]{2,1,0:T(8,128)(2,1)}, u32[]{:S(2)}) copy-start(bf16[1,1024,256]{2,1,0:T(8,128)(2,1)} %param.17) | copy-start | bytes 1572868
  13.6 42.0 %all-to-all-start.1 = ((bf16[4,1,1024,256]{3,2,1,0:T(8,128)(2,1)}), bf16[4,1,1024,256]{3,2,1,0:T(8,128)(2,1)S(1)}, u32[]{:S(2)}, u32[]{:S(2)}) async-start(bf16[4,1,1024,256]{3,2,1,0:T(8,128)(2,1)} %stack.3), calls=%async_computation.1 | async-start | bytes 4194304 | tf_op jit(solution)/shard_map/all_to_all | solution.py:90
  18.7 7.6 %copy-start.7 = (s32[3,2,256]{2,1,0:T(2,128)S(1)}, s32[3,2,256]{2,1,0:T(2,128)}, u32[]{:S(2)}) copy-start(s32[3,2,256]{2,1,0:T(2,128)} %param.18) | copy-start | bytes 18436
  18.7 7.6 %copy-start.5 = (s32[64,3]{0,1:T(4,128)S(1)}, s32[64,3]{0,1:T(4,128)}, u32[]{:S(2)}) copy-start(s32[64,3]{0,1:T(4,128)} %param.11) | copy-start | bytes 2308
  55.6 374.7 %all-to-all-start = ((bf16[3,4,256,256]{3,2,0,1:T(8,128)(2,1)}), bf16[3,4,256,256]{3,2,0,1:T(8,128)(2,1)}, u32[]{:S(2)}, u32[]{:S(2)}) async-start(bf16[3,4,256,256]{3,2,0,1:T(8,128)(2,1)} %copy.20), calls=%async_computation | async-start | bytes 3145728 | tf_op jit(solution)/shard_map/all_to_all | solution.py:98
  83.0 2.0 copy-start.2
  400.8 5.6 %copy-start.1 = (f32[1024,1024]{1,0:T(8,128)S(1)}, f32[1024,1024]{1,0:T(8,128)}, u32[]{:S(2)}) copy-start(f32[1024,1024]{1,0:T(8,128)} %fusion.43) | copy-start | bytes 12582916
  450.5 1.1 copy-start.3
  454.0 56.4 %all-to-all-start.2 = ((bf16[3,4,64,1024]{3,1,0,2:T(4,128)(2,1)}), bf16[3,4,64,1024]{3,1,0,2:T(4,128)(2,1)}, u32[]{:S(2)}, u32[]{:S(2)}) async-start(bf16[3,4,64,1024]{3,1,0,2:T(4,128)(2,1)} %copy.24), calls=%async_computation.2 | async-start | bytes 3145728 | tf_op jit(solution)/shard_map/all_to_all | solution.py:123
  470.7 44.4 %all-gather.5.cloned.1.call-start = ((), (), s32[]{:S(2)}) async-start(), calls=%async_computation.4 | async-start | bytes 1310720 | tf_op jit(solution)/shard_map/all_gather | solution.py:39
  515.0 5.9 %copy-start.4 = (f32[128,1,4,1,512]{4,3,2,1,0:T(1,128)S(1)}, f32[128,1,4,1,512]{4,3,2,1,0:T(1,128)}, u32[]{:S(2)}) copy-start(f32[128,1,4,1,512]{4,3,2,1,0:T(1,128)} %param.21) | copy-start | bytes 3145732
Sparse Core Ops, SparseCore 0:
  10.4 51.6 all-gather.2
  477.6 28.0 all-gather.4
